TPU v7x, 32 devices: a whole 2x2x4 slice. The times are simulated.
32 devices in a mesh: row: 4 (over z), col: 2 (over x), depth: 4 (over y, core).
Axes of the slice: x: 2, y: 2, z: 4, core: 2. Of those that a mesh axis runs over, the one named last changes fastest.
Arguments:
- tokens: bfloat16 [2560, 8192], P(('row', 'depth'), 'col'), may hold values from -6 to 6
- weight: bfloat16 [8192, 4096], P('row', 'col'), may hold values from -0.0625 to 0.0625
- cotangent: bfloat16 [2560, 4096], P(('row', 'depth'), 'col'), may hold values from -6 to 6
- master: float32 [8192, 4096], P(('row', 'depth'), 'col'), may hold values from -0.1 to 0.1
- first_moment: float32 [8192, 4096], P(('row', 'depth'), 'col'), may hold values from -6 to 6
- second_moment: float32 [8192, 4096], P(('row', 'depth'), 'col'), may hold values from 0.1 to 10
Outputs:
- queries: bfloat16 [2560, 4096], P(('row', 'depth'), 'col')
- token_grad: bfloat16 [2560, 8192], P(('row', 'depth'), 'col')
- new_master: float32 [8192, 4096], P(('row', 'depth'), 'col')
- new_first: float32 [8192, 4096], P(('row', 'depth'), 'col')
- new_second: float32 [8192, 4096], P(('row', 'depth'), 'col')
- new_weight: bfloat16 [8192, 4096], P('row', 'col')
All inputs are finite; a program needn't handle non-finite values.
Results may differ from a plain program's by a relative error of at most 0.001.
Values may be sent and summed in bfloat16 or wider, within the bound.
A program may use at most 128 MiB of HBM per device.

v0:
```python
import math
import jax
import jax.numpy as jnp
from jax import lax
from jax.sharding import PartitionSpec as P

beta_one = 0.9
beta_two = 0.95
learn_rate = 0.02
decay_rate = 0.1
adam_eps = 1e-08
bias_one = 1.0 - 0.9**50
bias_two = 1.0 - 0.95**50


def local(tokens, weight, cotangent, master, first_moment, second_moment):
    total_tokens = tokens.shape[0] * lax.axis_size("row") * lax.axis_size("depth")
    grad_scale = 1.0 / math.sqrt(total_tokens)
    full_rows = lax.all_gather(tokens, "col", axis=1, tiled=True)
    full_panel = lax.all_gather(weight, "row", axis=0, tiled=True)
    queries = jnp.dot(full_rows, full_panel, preferred_element_type=jnp.float32).astype(
        jnp.bfloat16
    )
    partial_value = lax.dot_general(
        cotangent, full_panel, (((1,), (1,)), ((), ())), preferred_element_type=jnp.float32
    )
    token_grad = lax.psum_scatter(partial_value, "col", scatter_dimension=1, tiled=True).astype(
        jnp.bfloat16
    )
    token_slab = lax.all_to_all(
        full_rows, ("row", "depth"), split_axis=1, concat_axis=0, tiled=True
    )
    product = lax.dot_general(
        token_slab,
        lax.all_gather(cotangent, ("row", "depth"), axis=0, tiled=True),
        (((0,), (0,)), ((), ())),
        preferred_element_type=jnp.float32,
    )
    grad = product * grad_scale
    new_first = beta_one * first_moment + (1.0 - beta_one) * grad
    new_second = beta_two * second_moment + (1.0 - beta_two) * grad * grad
    step_value = new_first / bias_one / (jnp.sqrt(new_second / bias_two) + adam_eps)
    new_master = master - learn_rate * (step_value + decay_rate * master)
    shard_weight = new_master.astype(jnp.bfloat16)
    new_weight = lax.all_gather(shard_weight, "depth", axis=0, tiled=True)
    return (queries, token_grad, new_master, new_first, new_second, new_weight)


def solution(mesh):
    in_specs = (
        P(("row", "depth"), "col"),
        P("row", "col"),
        P(("row", "depth"), "col"),
        P(("row", "depth"), "col"),
        P(("row", "depth"), "col"),
        P(("row", "depth"), "col"),
    )
    out_specs = (
        P(("row", "depth"), "col"),
        P(("row", "depth"), "col"),
        P(("row", "depth"), "col"),
        P(("row", "depth"), "col"),
        P(("row", "depth"), "col"),
        P("row", "col"),
    )
    return jax.shard_map(local, mesh=mesh, in_specs=in_specs, out_specs=out_specs, check_vma=False)
```

profile of v0, /device:TPU:0, one launch (start us, length us, event | category | flops | bytes accessed | tf_op | source)
XLA Modules:
  0.0 889.6 jit_solution(17956850485688772737)
XLA Ops:
  7.2 0.0 all-gather.5.cloned.1.call-start
  7.2 0.7 all-gather.5.cloned.1.call-update
  7.9 0.0 all-gather.9.cloned.1.call-start
  7.9 0.7 all-gather.9.cloned.1.call-update
  8.6 0.0 all-gather.7.cloned.1.call-start
  8.7 0.7 all-gather.7.cloned.1.call-update
  9.4 0.0 all-gather.11.cloned.1.call-start
  9.4 41.8 %all-gather.5.cloned.1.call-done = bf16[160,8192]{1,0:T(8,128)(2,1)} async-done(((bf16[160,4096]{1,0:T(8,128)(2,1)}), bf16[160,8192]{1,0:T(8,128)(2,1)}) %all-gather.5.cloned.1.call-update) | async-done | bytes 2621456 | tf_op jit(solution)/shard_map/all_gather | solution.py:19
  51.3 2.0 copy.16
  53.3 113.0 %all_to_all.19 = bf16[160,16,512]{2,0,1:T(8,128)(2,1)S(1)} all-to-all(bf16[160,16,512]{2,0,1:T(8,128)(2,1)S(1)} %bitcast.13), channel_id=1, replica_groups=mesh['row'=4,'col'=2,'depth'=4] {'row','depth'}, dimensions={1} | all-to-all | bytes 5242880 | tf_op jit(solution)/shard_map/all_to_all | solution.py:30
  166.3 17.8 %all-gather.9.cloned.1.call-done = bf16[2560,2048]{1,0:T(8,128)(2,1)} async-done(((bf16[160,2048]{1,0:T(8,128)(2,1)}), bf16[2560,2048]{1,0:T(8,128)(2,1)}) %all-gather.9.cloned.1.call-update) | async-done | bytes 10485776 | tf_op jit(solution)/shard_map/all_gather | solution.py:35
  184.1 0.0 copy-start
  184.1 18.9 %fusion = (bf16[512,2048]{1,0:T(8,128)(2,1)}, f32[512,2048]{1,0:T(8,128)}, f32[512,2048]{1,0:T(8,128)}, f32[512,2048]{1,0:T(8,128)}) fusion(f32[512,2048]{1,0:T(8,128)} %param.9, f32[512,2048]{1,0:T(8,128)} %param.10, f32[512,2048]{1,0:T(8,128)} %param.11, bf16[2560,512]{1,0:T(8,128)(2,1)S(1)} %bitcast.15, bf16[2560,2048]{1,0:T(8,128)(2,1)} %all-gather.9.cloned.1.call-done), kind=kOutput, calls=%fused_computation.5 | convolution fusion | flops 5386534912 | bytes 40370176 | tf_op jit(solution)/shard_map/dot_general | solution.py:33
  203.0 0.0 all-gather.11.cloned.1.call-update
  203.0 0.0 reduce-scatter.2.cloned.1.call-start
  203.1 542.1 %all-gather.7.cloned.1.call-done = bf16[8192,2048]{1,0:T(8,128)(2,1)} async-done(((bf16[2048,2048]{1,0:T(8,128)(2,1)}), bf16[8192,2048]{1,0:T(8,128)(2,1)}) %all-gather.7.cloned.1.call-update) | async-done | bytes 33554448 | tf_op jit(solution)/shard_map/all_gather | solution.py:20
  745.2 0.0 copy-done
  745.2 19.8 %fusion.1 = f32[160,8192]{1,0:T(8,128)} fusion(bf16[160,2048]{1,0:T(8,128)(2,1)S(1)} %copy-done, bf16[8192,2048]{1,0:T(8,128)(2,1)} %all-gather.7.cloned.1.call-done), kind=kOutput, calls=%fused_computation.6 | convolution fusion | flops 5368709120 | bytes 39452672 | tf_op jit(solution)/shard_map/dot_general | solution.py:24
  765.0 0.0 copy-start.1
  765.0 0.0 reduce-scatter.2.cloned.1.call-update
  765.1 38.1 %all-gather.11.cloned.1.call-done = bf16[2048,2048]{1,0:T(8,128)(2,1)} async-done(((bf16[512,2048]{1,0:T(8,128)(2,1)}), bf16[2048,2048]{1,0:T(8,128)(2,1)}) %all-gather.11.cloned.1.call-update) | async-done | bytes 8388624 | tf_op jit(solution)/shard_map/all_gather | solution.py:45
  803.1 0.0 copy-done.1
  803.1 15.2 %convolution_convert_fusion = bf16[160,2048]{1,0:T(8,128)(2,1)} fusion(bf16[160,8192]{1,0:T(8,128)(2,1)S(1)} %copy-done.1, bf16[8192,2048]{1,0:T(8,128)(2,1)} %all-gather.7.cloned.1.call-done), kind=kOutput, calls=%fused_computation.4 | convolution fusion | flops 5369036800 | bytes 36831232 | tf_op jit(solution)/shard_map/dot_general | solution.py:21
  818.3 53.3 %reduce-scatter.2.cloned.1.call-done = f32[160,4096]{1,0:T(8,128)} async-done(((f32[160,8192]{1,0:T(8,128)}), f32[160,4096]{1,0:T(8,128)}) %reduce-scatter.2.cloned.1.call-update) | async-done | bytes 2621456 | tf_op jit(solution)/shard_map/reduce_scatter | solution.py:27
  871.6 3.0 convert_element_type.10
  874.6 8.4 copy.18
Async XLA Ops:
  7.2 44.1 %all-gather.5.cloned.1.call-start = ((), (), s32[]{:S(2)}) async-start(), calls=%async_computation.2 | async-start | bytes 3932160 | tf_op jit(solution)/shard_map/all_gather | solution.py:19
  7.9 176.2 %all-gather.9.cloned.1.call-start = ((), (), s32[]{:S(2)}) async-start(), calls=%async_computation.5 | async-start | bytes 11141120 | tf_op jit(solution)/shard_map/all_gather | solution.py:35
  8.6 736.6 %all-gather.7.cloned.1.call-start = ((), (), s32[]{:S(2)}) async-start(), calls=%async_computation.3 | async-start | bytes 41943040 | tf_op jit(solution)/shard_map/all_gather | solution.py:20
  9.4 793.7 %all-gather.11.cloned.1.call-start = ((), (), s32[]{:S(2)}) async-start(), calls=%async_computation.6 | async-start | bytes 10485760 | tf_op jit(solution)/shard_map/all_gather | solution.py:45
  184.1 561.1 %copy-start = (bf16[160,2048]{1,0:T(8,128)(2,1)S(1)}, bf16[160,2048]{1,0:T(8,128)(2,1)}, u32[]{:S(2)}) copy-start(bf16[160,2048]{1,0:T(8,128)(2,1)} %param.8) | copy-start | bytes 1966084
  203.0 668.6 %reduce-scatter.2.cloned.1.call-start = ((), (), s32[]{:S(2)}) async-start(), calls=%async_computation.4 | async-start | bytes 7864320 | tf_op jit(solution)/shard_map/reduce_scatter | solution.py:27
  765.0 38.1 %copy-start.1 = (bf16[160,8192]{1,0:T(8,128)(2,1)S(1)}, bf16[160,8192]{1,0:T(8,128)(2,1)}, u32[]{:S(2)}) copy-start(bf16[160,8192]{1,0:T(8,128)(2,1)} %all-gather.5.cloned.1.call-done) | copy-start | bytes 7864324
Sparse Core Ops, SparseCore 0:
  9.5 41.7 all-gather.4
  53.6 130.5 all-gather.8
  185.7 559.5 all-gather.6
  746.6 56.4 all-gather.10
  805.8 65.7 reduce-scatter.1
where the time goes:
time: 890 us
  waiting for transfers between devices  695 us (78%)
  blocking collectives  113 us (13%)
  matrix products  53.9 us (6%)
  between operations  13.8 us (2%)
  local copies, waits for them, and re-layouts  10.4 us (1%)
    all_gather x1, waiting for transfers between devices, local(): full_panel = lax.all_gather(weight, 'row', axis=0, tiled=True)  542 us
    all_to_all x1, blocking collectives, local(): lax.all_to_all(full_rows, ('row', 'depth'), split_axis=1, concat_axis=0,...  113 us
    reduce_scatter x1, waiting for transfers between devices, local(): lax.psum_scatter(partial_value, 'col', scatter_dimension=1, tiled=True)  53.3 us
    all_gather x1, waiting for transfers between devices, local(): full_rows = lax.all_gather(tokens, 'col', axis=1, tiled=True)  41.8 us
    all_gather x1, waiting for transfers between devices, local(): new_weight = lax.all_gather(shard_weight, 'depth', axis=0, tiled=True)  38.1 us
    dot_general x1, matrix products, local(): lax.dot_general(cotangent, full_panel, (((1,), (1,)), ((), ())), preferre...  19.8 us
    dot_general x1, matrix products, local(): lax.dot_general(token_slab, lax.all_gather(cotangent, ('row', 'depth'), a...  18.9 us
    all_gather x1, waiting for transfers between devices, local(): lax.all_gather(cotangent, ('row', 'depth'), axis=0, tiled=True)  17.8 us
  transfers between devices with their start and end apart: 5, of which 5 were waited for; matrix products, arithmetic and copies ran while one was open for 6% of the time, Pallas kernels for 0%

commit v1 on v0

--- a/solution.py
+++ b/solution.py
@@ -27,9 +27,10 @@
     token_grad = lax.psum_scatter(partial_value, "col", scatter_dimension=1, tiled=True).astype(
         jnp.bfloat16
     )
-    token_slab = lax.all_to_all(
-        full_rows, ("row", "depth"), split_axis=1, concat_axis=0, tiled=True
-    )
+    size = lax.axis_size(("row", "depth"))
+    tiles = jnp.stack(jnp.split(full_rows, size, axis=1), axis=0)
+    tiles = lax.all_to_all(tiles, ("row", "depth"), split_axis=0, concat_axis=0)
+    token_slab = jnp.concatenate(tiles, axis=0)
     product = lax.dot_general(
         token_slab,
         lax.all_gather(cotangent, ("row", "depth"), axis=0, tiled=True),

time: 890 us -> 894 us (level)
  transfers between devices with their start and end apart: 5 -> 5, of which waited for: 5 -> 5; matrix products, arithmetic and copies ran while one was open for 6% -> 7% of each run, Pallas kernels for 0% -> 0%
where the time goes in v1:
time: 894 us
  waiting for transfers between devices  689 us (77%)
  blocking collectives  117 us (13%)
  matrix products  53.2 us (6%)
  local copies, waits for them, and re-layouts  17 us (2%)
  between operations  13.9 us (2%)
    all_gather x1, waiting for transfers between devices, local(): full_panel = lax.all_gather(weight, 'row', axis=0, tiled=True)  544 us
    all_to_all x1, blocking collectives, local(): tiles = lax.all_to_all(tiles, ('row', 'depth'), split_axis=0, concat_axis=0)  117 us
    reduce_scatter x1, waiting for transfers between devices, local(): lax.psum_scatter(partial_value, 'col', scatter_dimension=1, tiled=True)  53.3 us
    all_gather x1, waiting for transfers between devices, local(): full_rows = lax.all_gather(tokens, 'col', axis=1, tiled=True)  41.8 us
    all_gather x1, waiting for transfers between devices, local(): new_weight = lax.all_gather(shard_weight, 'depth', axis=0, tiled=True)  38.1 us
    dot_general x1, matrix products, local(): lax.dot_general(cotangent, full_panel, (((1,), (1,)), ((), ())), preferre...  19.8 us
    dot_general x1, matrix products, local(): lax.dot_general(token_slab, lax.all_gather(cotangent, ('row', 'depth'), a...  18.2 us
  transfers between devices with their start and end apart: 5, of which 5 were waited for; matrix products, arithmetic and copies ran while one was open for 7% of the time, Pallas kernels for 0%

profile of v1, /device:TPU:0, one launch (start us, length us, event | category | flops | bytes accessed | tf_op | source)
XLA Modules:
  0.0 893.6 jit_solution(17808362248447207647)
XLA Ops:
  7.2 0.0 all-gather.5.cloned.1.call-start
  7.2 0.7 all-gather.5.cloned.1.call-update
  7.9 0.0 all-gather.9.cloned.1.call-start
  7.9 0.7 all-gather.9.cloned.1.call-update
  8.6 0.0 all-gather.7.cloned.1.call-start
  8.7 0.7 all-gather.7.cloned.1.call-update
  9.4 0.0 all-gather.11.cloned.1.call-start
  9.4 41.8 %all-gather.5.cloned.1.call-done = bf16[160,8192]{1,0:T(8,128)(2,1)} async-done(((bf16[160,4096]{1,0:T(8,128)(2,1)}), bf16[160,8192]{1,0:T(8,128)(2,1)}) %all-gather.5.cloned.1.call-update) | async-done | bytes 2621456 | tf_op jit(solution)/shard_map/all_gather | solution.py:19
  51.3 0.0 copy-start.1
  51.3 1.1 fusion.15
  52.4 0.9 fusion.14
  53.3 0.9 fusion.13
  54.2 0.9 fusion.12
  55.1 0.9 fusion.11
  56.1 0.9 fusion.10
  57.0 0.9 fusion.9
  57.9 0.9 fusion.8
  58.9 0.9 fusion.7
  59.8 0.0 copy-done.1
  60.0 117.0 %all_to_all.5 = bf16[16,160,512]{2,1,0:T(8,128)(2,1)} all-to-all(bf16[16,160,512]{2,1,0:T(8,128)(2,1)S(1)} %fusion), channel_id=1, replica_groups=mesh['row'=4,'col'=2,'depth'=4] {'row','depth'}, dimensions={0} | all-to-all | bytes 5242880 | tf_op jit(solution)/shard_map/all_to_all | solution.py:32
  177.0 10.4 %all-gather.9.cloned.1.call-done = bf16[2560,2048]{1,0:T(8,128)(2,1)} async-done(((bf16[160,2048]{1,0:T(8,128)(2,1)}), bf16[2560,2048]{1,0:T(8,128)(2,1)}) %all-gather.9.cloned.1.call-update) | async-done | bytes 10485776 | tf_op jit(solution)/shard_map/all_gather | solution.py:36
  187.4 18.2 %fusion.16 = (bf16[512,2048]{1,0:T(8,128)(2,1)}, f32[512,2048]{1,0:T(8,128)}, f32[512,2048]{1,0:T(8,128)}, f32[512,2048]{1,0:T(8,128)}) fusion(f32[512,2048]{1,0:T(8,128)} %param.9, f32[512,2048]{1,0:T(8,128)} %param.10, f32[512,2048]{1,0:T(8,128)} %param.11, bf16[2560,512]{1,0:T(8,128)(2,1)} %bitcast.71, bf16[2560,2048]{1,0:T(8,128)(2,1)} %all-gather.9.cloned.1.call-done), kind=kOutput, calls=%fused_computation.36 | convolution fusion | flops 5386534912 | bytes 40370176 | tf_op jit(solution)/shard_map/dot_general | solution.py:34
  205.6 0.0 copy-start
  205.6 0.0 all-gather.11.cloned.1.call-update
  205.6 0.0 reduce-scatter.2.cloned.1.call-start
  205.7 543.6 %all-gather.7.cloned.1.call-done = bf16[8192,2048]{1,0:T(8,128)(2,1)} async-done(((bf16[2048,2048]{1,0:T(8,128)(2,1)}), bf16[8192,2048]{1,0:T(8,128)(2,1)}) %all-gather.7.cloned.1.call-update) | async-done | bytes 33554448 | tf_op jit(solution)/shard_map/all_gather | solution.py:20
  749.3 0.0 copy-done
  749.3 19.8 %fusion.17 = f32[160,8192]{1,0:T(8,128)} fusion(bf16[160,2048]{1,0:T(8,128)(2,1)S(1)} %copy-done, bf16[8192,2048]{1,0:T(8,128)(2,1)} %all-gather.7.cloned.1.call-done), kind=kOutput, calls=%fused_computation.37 | convolution fusion | flops 5368709120 | bytes 39452672 | tf_op jit(solution)/shard_map/dot_general | solution.py:24
  769.1 0.0 reduce-scatter.2.cloned.1.call-update
  769.1 38.1 %all-gather.11.cloned.1.call-done = bf16[2048,2048]{1,0:T(8,128)(2,1)} async-done(((bf16[512,2048]{1,0:T(8,128)(2,1)}), bf16[2048,2048]{1,0:T(8,128)(2,1)}) %all-gather.11.cloned.1.call-update) | async-done | bytes 8388624 | tf_op jit(solution)/shard_map/all_gather | solution.py:46
  807.2 15.2 %convolution_convert_fusion = bf16[160,2048]{1,0:T(8,128)(2,1)} fusion(bf16[160,8192]{1,0:T(8,128)(2,1)S(1)} %copy-done.1, bf16[8192,2048]{1,0:T(8,128)(2,1)} %all-gather.7.cloned.1.call-done), kind=kOutput, calls=%fused_computation.3 | convolution fusion | flops 5369036800 | bytes 36831232 | tf_op jit(solution)/shard_map/dot_general | solution.py:21
  822.4 53.3 %reduce-scatter.2.cloned.1.call-done = f32[160,4096]{1,0:T(8,128)} async-done(((f32[160,8192]{1,0:T(8,128)}), f32[160,4096]{1,0:T(8,128)}) %reduce-scatter.2.cloned.1.call-update) | async-done | bytes 2621456 | tf_op jit(solution)/shard_map/reduce_scatter | solution.py:27
  875.7 3.0 convert_element_type.10
  878.6 8.4 copy.28
  (7 shorter events, 0.1 us)
Async XLA Ops:
  7.2 44.1 %all-gather.5.cloned.1.call-start = ((), (), s32[]{:S(2)}) async-start(), calls=%async_computation.2 | async-start | bytes 3932160 | tf_op jit(solution)/shard_map/all_gather | solution.py:19
  7.9 179.5 %all-gather.9.cloned.1.call-start = ((), (), s32[]{:S(2)}) async-start(), calls=%async_computation.5 | async-start | bytes 11141120 | tf_op jit(solution)/shard_map/all_gather | solution.py:36
  8.6 740.6 %all-gather.7.cloned.1.call-start = ((), (), s32[]{:S(2)}) async-start(), calls=%async_computation.3 | async-start | bytes 41943040 | tf_op jit(solution)/shard_map/all_gather | solution.py:20
  9.4 797.8 %all-gather.11.cloned.1.call-start = ((), (), s32[]{:S(2)}) async-start(), calls=%async_computation.6 | async-start | bytes 10485760 | tf_op jit(solution)/shard_map/all_gather | solution.py:46
  51.3 8.5 copy-start.1
  205.6 543.7 %copy-start = (bf16[160,2048]{1,0:T(8,128)(2,1)S(1)}, bf16[160,2048]{1,0:T(8,128)(2,1)}, u32[]{:S(2)}) copy-start(bf16[160,2048]{1,0:T(8,128)(2,1)} %param.8) | copy-start | bytes 1966084
  205.6 670.1 %reduce-scatter.2.cloned.1.call-start = ((), (), s32[]{:S(2)}) async-start(), calls=%async_computation.4 | async-start | bytes 7864320 | tf_op jit(solution)/shard_map/reduce_scatter | solution.py:27
Sparse Core Ops, SparseCore 0:
  9.5 41.7 all-gather.4
  53.6 133.7 all-gather.8
  188.9 560.2 all-gather.6
  750.7 56.4 all-gather.10
  809.9 65.7 reduce-scatter.1
